TPU v7x, 256 devices: a whole 4x4x8 slice. The times are simulated.
256 devices in a mesh: section: 8 (over y, x_hi), ctx: 32 (over x_lo, z, core).
Axes of the slice: x: 4 (x_hi: 2, x_lo: 2; x = x_hi * 2 + x_lo), y: 4, z: 8, core: 2. Of those that a mesh axis runs over, the one named last changes fastest.
Arguments:
- queries: bfloat16 [8, 12288, 40, 128], P('section', 'ctx'), may hold values from -60 to 60
- keys_values: bfloat16 [12288, 2, 40, 128], P('ctx', None, 'section'), may hold values from -6 to 6
- positions: int32 [12288], P('ctx'), may hold values from 0 to 1533, as said below
- documents: int32 [12288], P('ctx'), may hold values from 0 to 12287, as said below
Outputs:
- attended: bfloat16 [8, 12288, 40, 128], P('section', 'ctx')
Inputs may be any that keep to these rules, and one draw needn't show every extreme that they name: `documents`: Non-decreasing along the sequence; each document is a run of 1 to 384 tokens sharing one id, one document has exactly 384 tokens, and the last document's id is 12287. `positions`: within a document the ids rise by 1 to 3 from each token to the next; a document's first id is 0 to 384.
All inputs are finite; a program needn't handle non-finite values.
Results may differ from a plain program's by a relative error of at most 0.01.
Values may be sent and summed in bfloat16 or wider, within the bound.
A program may use at most 128 MiB of HBM per device.

v0:
```python
import jax
import jax.numpy as jnp
from jax import lax
from jax.sharding import PartitionSpec as P


def shifted(block, axis, distance):
    devices = range(lax.axis_size(axis))
    route = [(i - distance, i) for i in devices if i - distance in devices]
    return lax.ppermute(block, axis, route)


def rotate(values, token_positions):
    half_dim = values.shape[-1] // 2
    exponent = jnp.arange(half_dim, dtype=jnp.float32) * (2.0 / values.shape[-1])
    inverse = jnp.power(jnp.float32(10000.0), -exponent)
    angles = token_positions.astype(jnp.float32)[:, None] * inverse[None, :]
    cosine = jnp.cos(angles)[:, None, :]
    sine = jnp.sin(angles)[:, None, :]
    widened = values.astype(jnp.float32)
    lower = widened[..., :half_dim]
    upper = widened[..., half_dim:]
    joined = jnp.concatenate(
        [lower * cosine - upper * sine, upper * cosine + lower * sine], axis=-1
    )
    return joined.astype(jnp.bfloat16)


def attend(rotated, piece, key_docs, query_docs):
    query_rows = query_docs.shape[0]
    key_rows = key_docs.shape[0]
    head_count = piece.shape[2]
    head_dim = piece.shape[3]
    factor = max((option for option in range(1, 9) if head_count % option == 0))
    groups = head_count // factor

    def split_heads(values, length):
        return jnp.moveaxis(values.reshape(length, groups, factor, head_dim), 1, 0)

    allowed = jnp.logical_and(
        key_docs[None, :] == query_docs[:, None],
        jnp.arange(key_rows)[None, :] <= jnp.arange(query_rows)[:, None] + (key_rows - query_rows),
    )
    scale = head_dim ** (-0.5)

    def one_group(operands):
        query_part, key_part, value_part = operands
        scores = (
            jnp.einsum("qhd,khd->hqk", query_part, key_part, preferred_element_type=jnp.float32)
            * scale
        )
        scores = jnp.where(allowed[None], scores, -1e30)
        largest = jnp.max(scores, axis=-1, keepdims=True)
        weights = jnp.exp(scores - largest)
        probs = (weights / jnp.sum(weights, axis=-1, keepdims=True)).astype(jnp.bfloat16)
        mixed = jnp.einsum("hqk,khd->qhd", probs, value_part, preferred_element_type=jnp.float32)
        return mixed.astype(jnp.bfloat16)

    output = lax.map(
        one_group,
        (
            split_heads(rotated, query_rows),
            split_heads(piece[:, 0], key_rows),
            split_heads(piece[:, 1], key_rows),
        ),
    )
    return jnp.moveaxis(output, 0, 1).reshape(query_rows, head_count, head_dim)


def body(queries, keys_values, positions, documents):
    rotated = rotate(queries[0], positions)
    key_share = rotate(keys_values[:, 0], positions)
    share = jnp.stack([key_share, keys_values[:, 1]], axis=1)
    at_start = lax.axis_index("ctx") == 0
    whole = lax.all_gather(share, "section", axis=2, tiled=True)
    earlier, earlier_docs = shifted((whole, documents), "ctx", 1)
    key_docs = jnp.concatenate(
        [jnp.where(at_start, -1, earlier_docs).astype(jnp.int32), documents], axis=0
    )
    window = jnp.concatenate([earlier, whole], axis=0)
    result = attend(rotated, window, key_docs, documents)
    return result[None]


def solution(mesh):
    placed = (P("section", "ctx", None, None), P("ctx", None, "section", None), P("ctx"), P("ctx"))
    return jax.shard_map(
        body, mesh=mesh, in_specs=placed, out_specs=P("section", "ctx", None, None), check_vma=False
    )
```

profile of v0, /device:TPU:2, one launch (start us, length us, event | category | flops | bytes accessed | tf_op | source)
XLA Modules:
  0.0 344.2 jit_solution(13861718311189007667)
XLA Ops:
  7.2 3.3 fusion.33
  13.6 109.1 %all-gather.2.cloned.1.call-done = bf16[384,2,40,128]{0,3,2,1:T(8,128)(2,1)} async-done(((bf16[384,2,5,128]{0,3,2,1:T(8,128)(2,1)}), bf16[384,2,40,128]{0,3,2,1:T(8,128)(2,1)}) %all-gather.2.cloned.1.call-update) | async-done | bytes 7864336 | tf_op jit(solution)/shard_map/all_gather | solution.py:75
  124.6 3.6 %collective-permute-start.1 = (s32[384]{0:T(512)S(1)}, s32[384]{0:T(512)S(1)}, u32[]{:S(2)}, u32[]{:S(2)}) collective-permute-start(s32[384]{0:T(512)S(1)} %copy-done), channel_id=1, source_target_pairs={{0,1},{1,2},{2,3},{3,4},{4,5},{5,6},{6,7},{7,8},{8,9},{9,10},{10,1... | collective-permute-start | bytes 4616 | tf_op jit(solution)/shard_map/ppermute | solution.py:10
  135.6 4.1 %maximum_bitcast_fusion = bf16[5,384,8,128]{3,1,2,0:T(8,128)(2,1)} fusion(bf16[384,5,8,64]{3,0,2,1:T(8,128)(2,1)S(1)} %bitcast.53, bf16[384,5,8,64]{3,0,2,1:T(8,128)(2,1)S(1)} %bitcast.52), kind=kLoop, calls=%fused_computation.28 | loop fusion | flops 7864320 | bytes 7864320 | tf_op jit(solution)/shard_map/transpose | solution.py:38
  139.7 74.6 %collective-permute-done.1 = s32[384]{0:T(512)S(1)} collective-permute-done((s32[384]{0:T(512)S(1)}, s32[384]{0:T(512)S(1)}, u32[]{:S(2)}, u32[]{:S(2)}) %collective-permute-start.1) | collective-permute-done | bytes 1568 | tf_op jit(solution)/shard_map/ppermute | solution.py:10
  214.3 8.1 %constant_dynamic-update-slice_fusion.1 = bf16[768,2,40,128]{0,3,2,1:T(8,128)(2,1)} fusion(bf16[384,2,40,128]{0,3,2,1:T(8,128)(2,1)} %collective-permute-done), kind=kLoop, calls=%fused_computation.39 | loop fusion | bytes 15728640
  222.4 4.3 %constant_dynamic-update-slice_fusion = bf16[768,2,40,128]{0,3,2,1:T(8,128)(2,1)} fusion(bf16[768,2,40,128]{0,3,2,1:T(8,128)(2,1)} %constant_dynamic-update-slice_fusion.1, bf16[384,2,40,128]{0,3,2,1:T(8,128)(2,1)S(1)} %bitcast.55), kind=kLoop, calls=%fused_computation.38 | loop fusion | bytes 15728640 | tf_op jit(solution)/shard_map/concatenate | solution.py:80
  226.7 11.1 %fusion.32 = (bf16[768,1,40,128]{0,3,2,1:T(8,128)(2,1)}, bf16[768,1,40,128]{0,3,2,1:T(8,128)(2,1)}) fusion(bf16[768,2,40,128]{0,3,2,1:T(8,128)(2,1)} %constant_dynamic-update-slice_fusion), kind=kLoop, calls=%fused_computation.45 | loop fusion | bytes 31457280 | tf_op jit(solution)/shard_map/slice | solution.py:63
  237.8 10.6 %copy.18 = bf16[768,5,8,128]{3,0,2,1:T(8,128)(2,1)} copy(bf16[768,5,8,128]{0,3,2,1:T(8,128)(2,1)} %bitcast.51) | data formatting | bytes 15728640 | tf_op jit(solution)/shard_map/reshape;squeeze | solution.py:38
  248.4 82.5 %while.11 = (s32[]{:T(128)}, bf16[5,384,8,128]{1,3,2,0:T(8,128)(2,1)}, bf16[5,768,8,128]{1,3,2,0:T(8,128)(2,1)}, bf16[5,384,8,128]{3,1,2,0:T(8,128)(2,1)}, bf16[...) while((s32[]{:T(128)}, ...), condition=%wide.region_3.4_spmd.clone, body=%wide.region_0.3_spmd.clone.sunk | while | flops 1228112640 | bytes 43090012 | solution.py:59
  248.4 3.0 fusion.44
  251.9 6.5 %fusion.46 = (f32[8,384]{1,0:T(8,128)S(1)}, f32[8,384,768]{2,1,0:T(8,128)}) fusion(f32[8,384,768]{2,1,0:T(8,128)S(1)} %fusion.44, pred[384,768]{1,0:T(8,128)(4,1)S(1)} %fusion.45), kind=kOutput, calls=%fused_computation.44.clone.1 | output fusion | flops 14156543 | bytes 19181568 | tf_op jit(solution)/shard_map/while/body/eval_jaxpr/sub | solution.py:54
  258.3 6.6 %fusion.47 = bf16[5,384,8,128]{1,3,2,0:T(8,128)(2,1)} fusion(bf16[5,384,8,128]{1,3,2,0:T(8,128)(2,1)} %get-tuple-element.150, s32[]{:T(128)} %get-tuple-element.149, f32[8,384,768]{2,1,0:T(8,128)} %get-tuple-element.138, f32[8,384]{1,0:T(8,128)S(1)} %get-tuple-element.139, bf16[5,768,8,128]{1,3,2,0:T(8,128)(2,1)} %get-tuple-element.160), kind=kOutput, calls=%fused_computation.17.clone.1 | convolution fusion | flops 609091584 | bytes 11809792 | tf_op jit(solution)/shard_map/while/body/eval_jaxpr/hqk,khd->qhd/dot_general | solution.py:56
  268.4 6.5 %fusion.46 = (f32[8,384]{1,0:T(8,128)S(1)}, f32[8,384,768]{2,1,0:T(8,128)}) fusion(f32[8,384,768]{2,1,0:T(8,128)S(1)} %fusion.44, pred[384,768]{1,0:T(8,128)(4,1)S(1)} %fusion.45), kind=kOutput, calls=%fused_computation.44.clone.1 | output fusion | flops 14156543 | bytes 19181568 | tf_op jit(solution)/shard_map/while/body/eval_jaxpr/sub | solution.py:54
  274.9 6.6 %fusion.47 = bf16[5,384,8,128]{1,3,2,0:T(8,128)(2,1)} fusion(bf16[5,384,8,128]{1,3,2,0:T(8,128)(2,1)} %get-tuple-element.150, s32[]{:T(128)} %get-tuple-element.149, f32[8,384,768]{2,1,0:T(8,128)} %get-tuple-element.138, f32[8,384]{1,0:T(8,128)S(1)} %get-tuple-element.139, bf16[5,768,8,128]{1,3,2,0:T(8,128)(2,1)} %get-tuple-element.160), kind=kOutput, calls=%fused_computation.17.clone.1 | convolution fusion | flops 609091584 | bytes 11809792 | tf_op jit(solution)/shard_map/while/body/eval_jaxpr/hqk,khd->qhd/dot_general | solution.py:56
  281.5 3.0 fusion.44
  284.9 6.5 %fusion.46 = (f32[8,384]{1,0:T(8,128)S(1)}, f32[8,384,768]{2,1,0:T(8,128)}) fusion(f32[8,384,768]{2,1,0:T(8,128)S(1)} %fusion.44, pred[384,768]{1,0:T(8,128)(4,1)S(1)} %fusion.45), kind=kOutput, calls=%fused_computation.44.clone.1 | output fusion | flops 14156543 | bytes 19181568 | tf_op jit(solution)/shard_map/while/body/eval_jaxpr/sub | solution.py:54
  291.4 6.5 %fusion.47 = bf16[5,384,8,128]{1,3,2,0:T(8,128)(2,1)} fusion(bf16[5,384,8,128]{1,3,2,0:T(8,128)(2,1)} %get-tuple-element.150, s32[]{:T(128)} %get-tuple-element.149, f32[8,384,768]{2,1,0:T(8,128)} %get-tuple-element.138, f32[8,384]{1,0:T(8,128)S(1)} %get-tuple-element.139, bf16[5,768,8,128]{1,3,2,0:T(8,128)(2,1)} %get-tuple-element.160), kind=kOutput, calls=%fused_computation.17.clone.1 | convolution fusion | flops 609091584 | bytes 11809792 | tf_op jit(solution)/shard_map/while/body/eval_jaxpr/hqk,khd->qhd/dot_general | solution.py:56
  297.9 3.0 fusion.44
  301.3 6.5 %fusion.46 = (f32[8,384]{1,0:T(8,128)S(1)}, f32[8,384,768]{2,1,0:T(8,128)}) fusion(f32[8,384,768]{2,1,0:T(8,128)S(1)} %fusion.44, pred[384,768]{1,0:T(8,128)(4,1)S(1)} %fusion.45), kind=kOutput, calls=%fused_computation.44.clone.1 | output fusion | flops 14156543 | bytes 19181568 | tf_op jit(solution)/shard_map/while/body/eval_jaxpr/sub | solution.py:54
  307.8 6.7 %fusion.47 = bf16[5,384,8,128]{1,3,2,0:T(8,128)(2,1)} fusion(bf16[5,384,8,128]{1,3,2,0:T(8,128)(2,1)} %get-tuple-element.150, s32[]{:T(128)} %get-tuple-element.149, f32[8,384,768]{2,1,0:T(8,128)} %get-tuple-element.138, f32[8,384]{1,0:T(8,128)S(1)} %get-tuple-element.139, bf16[5,768,8,128]{1,3,2,0:T(8,128)(2,1)} %get-tuple-element.160), kind=kOutput, calls=%fused_computation.17.clone.1 | convolution fusion | flops 609091584 | bytes 11809792 | tf_op jit(solution)/shard_map/while/body/eval_jaxpr/hqk,khd->qhd/dot_general | solution.py:56
  317.9 6.5 %fusion.46 = (f32[8,384]{1,0:T(8,128)S(1)}, f32[8,384,768]{2,1,0:T(8,128)}) fusion(f32[8,384,768]{2,1,0:T(8,128)S(1)} %fusion.44, pred[384,768]{1,0:T(8,128)(4,1)S(1)} %fusion.45), kind=kOutput, calls=%fused_computation.44.clone.1 | output fusion | flops 14156543 | bytes 19181568 | tf_op jit(solution)/shard_map/while/body/eval_jaxpr/sub | solution.py:54
  324.4 6.6 %fusion.47 = bf16[5,384,8,128]{1,3,2,0:T(8,128)(2,1)} fusion(bf16[5,384,8,128]{1,3,2,0:T(8,128)(2,1)} %get-tuple-element.150, s32[]{:T(128)} %get-tuple-element.149, f32[8,384,768]{2,1,0:T(8,128)} %get-tuple-element.138, f32[8,384]{1,0:T(8,128)S(1)} %get-tuple-element.139, bf16[5,768,8,128]{1,3,2,0:T(8,128)(2,1)} %get-tuple-element.160), kind=kOutput, calls=%fused_computation.17.clone.1 | convolution fusion | flops 609091584 | bytes 11809792 | tf_op jit(solution)/shard_map/while/body/eval_jaxpr/hqk,khd->qhd/dot_general | solution.py:56
  331.0 6.4 %copy.19 = bf16[384,5,8,128]{3,2,1,0:T(8,128)(2,1)} copy(bf16[384,5,8,128]{0,3,2,1:T(8,128)(2,1)} %bitcast.13) | data formatting | bytes 7864320 | tf_op jit(solution)/shard_map/transpose | solution.py:67
  (36 shorter events, 20.9 us)
Async XLA Ops:
  6.5 118.1 %copy-start = (s32[384]{0:T(512)S(1)}, s32[384]{0:T(512)}, u32[]{:S(2)}) copy-start(s32[384]{0:T(512)} %param.9) | copy-start | bytes 4612
  6.5 116.1 %all-gather.2.cloned.1.call-start = ((), (), s32[]{:S(2)}) async-start(), calls=%async_computation | async-start | bytes 8847360 | tf_op jit(solution)/shard_map/all_gather | solution.py:75
  122.7 91.6 %collective-permute-start = (bf16[384,2,40,128]{0,3,2,1:T(8,128)(2,1)}, bf16[384,2,40,128]{0,3,2,1:T(8,128)(2,1)}, u32[]{:S(2)}, u32[]{:S(2)}) collective-permute-start(bf16[384,2,40,128]{0,3,2,1:T(8,128)(2,1)} %all-gather.2.cloned.1.call-done), channel_id=1, source_target_pairs={{0,1},{1,2},{2,3},{3,4},{4,5},{5,6},{6,7},{7,8},{8,9},{9,10},{10,1... | collective-permute-start | bytes 23592968 | tf_op jit(solution)/shard_map/ppermute | solution.py:10
  124.6 89.6 %collective-permute-start.1 = (s32[384]{0:T(512)S(1)}, s32[384]{0:T(512)S(1)}, u32[]{:S(2)}, u32[]{:S(2)}) collective-permute-start(s32[384]{0:T(512)S(1)} %copy-done), channel_id=1, source_target_pairs={{0,1},{1,2},{2,3},{3,4},{4,5},{5,6},{6,7},{7,8},{8,9},{9,10},{10,1... | collective-permute-start | bytes 4616 | tf_op jit(solution)/shard_map/ppermute | solution.py:10
  214.2 8.1 %slice-start = ((s8[7864320]{0:T(1024)(128)(4,1)}), s8[4194304]{0:T(1024)(128)(4,1)S(1)}, s32[]{:S(2)}) async-start(s8[7864320]{0:T(1024)(128)(4,1)} %bitcast.54), calls=%async_computation.1 | async-start | bytes 8388608
  214.3 8.1 %slice-start.1 = ((s8[7864320]{0:T(1024)(128)(4,1)}), s8[3670016]{0:T(1024)(128)(4,1)S(1)}, s32[]{:S(2)}) async-start(s8[7864320]{0:T(1024)(128)(4,1)} %bitcast.54), calls=%async_computation.2 | async-start | bytes 7340032
Sparse Core Ops, SparseCore 0:
  13.7 108.9 all-gather.1
where the time goes:
time: 345 us; the launch traced here: 344 us
  waiting for transfers between devices  184 us (53%)
  matrix products  48.2 us (14%)
  local copies, waits for them, and re-layouts  47.3 us (14%)
  other arithmetic  46 us (13%)
  between operations  13.5 us (4%)
  starting transfers between devices  5.48 us (2%)
    all_gather x1, waiting for transfers between devices, body(): whole = lax.all_gather(share, 'section', axis=2, tiled=True)  109 us
    ppermute x2, waiting for transfers between devices, shifted(): return lax.ppermute(block, axis, route)  74.6 us
    dot_general x5, matrix products, one_group(): jnp.einsum('hqk,khd->qhd', probs, value_part, preferred_element_type=jnp....  33 us
    sub x5, other arithmetic, one_group(): weights = jnp.exp(scores - largest)  32.5 us
    dot_general x5, matrix products, one_group(): jnp.einsum('qhd,khd->hqk', query_part, key_part, preferred_element_type=j...  15.2 us
    slice x1, local copies, waits for them, and re-layouts, attend(): piece[:, 0]  11.1 us
    another operation x1, local copies, waits for them, and re-layouts, split_heads(): return jnp.moveaxis(values.reshape(length, groups, factor, head_dim), 1, 0)  10.6 us
    unnamed x9, local copies, waits for them, and re-layouts  9.43 us
  transfers between devices with their start and end apart: 3, of which 2 were waited for; matrix products, arithmetic and copies ran while one was open for 3% of the time, Pallas kernels for 0%

commit v1 on v0

v1 whole, which is shorter than its diff:
```python
import functools

import jax
import jax.numpy as jnp
from jax import lax
from jax.experimental import pallas as pl
from jax.experimental.pallas import tpu as pltpu
from jax.sharding import PartitionSpec as P

MESH = pl.DeviceIdType.MESH
HOP = 1.8

OWN = ((0, 0, 3, 1, 1, 1), (0, 3, 2, 1, -1, -1), (1, 4, 1, 1, -1, -1), (1, 0, 2, 2, 1, 1), (1, 2, 2, 2, -1, -1))
PREV = ((0, 0, 3, 1, -1, -1), (0, 3, 2, 1, 1, 1), (1, 0, 3, 2, 1, 1), (1, 3, 2, 2, -1, -1))
CHUNKS = {"own": OWN, "prev": PREV}


def gather_tasks(core, stream, source_event):
    tasks = []

    def add(needs, link, units, event, what):
        tasks.append((core, needs, link, units, event, core, what))

    def along_y(chunk, units, turn, block, needs):
        for way in (turn, -turn):
            add(needs, ("y", way), units, (stream, "y1", way, block, chunk), ("ysend", stream, block, chunk, way))
        add(
            ((stream, "y1", turn, block, chunk),),
            ("y", turn),
            units,
            (stream, "y2", block, chunk),
            ("yfwd", stream, block, chunk, turn),
        )

    for chunk, (_, _, units, path, way, turn) in enumerate(CHUNKS[stream]):
        start = source_event(chunk)
        along_y(chunk, units, turn, 0, start)
        if path == 1:
            crossings = [(0, start, way)]
        else:
            crossings = [
                (0, start, way),
                (-1, ((stream, "y1", 1, 0, chunk),), -way),
                (2, ((stream, "y2", 0, chunk),), -way),
                (1, ((stream, "y1", -1, 0, chunk),), way),
            ]
        for row, needs, side in crossings:
            relay = (stream, "relay", row, chunk)
            add(needs, ("x", side), units, relay, ("xsend", stream, row, chunk, side))
            add((relay,), ("x", side), units, (stream, "x", row, chunk), ("xfwd", stream, row, chunk, side))
        if path == 1:
            along_y(chunk, units, turn, 1, ((stream, "x", 0, chunk),))
    return tasks


def all_tasks():
    tasks = gather_tasks(0, "own", lambda chunk: ()) + gather_tasks(1, "own", lambda chunk: ())
    for chunk, entry in enumerate(PREV):
        tasks.append((1, (), ("z", 1), entry[2], ("prev", "shift", chunk), 0, ("shift", "prev", chunk)))
    tasks += gather_tasks(0, "prev", lambda chunk: (("prev", "shift", chunk),))
    for chunk, (_, _, units, path, _, _) in enumerate(OWN):
        arrivals = [
            ((), 0, 0),
            ((("own", "y1", 1, 0, chunk),), -1, 0),
            ((("own", "y2", 0, chunk),), 2, 0),
            ((("own", "y1", -1, 0, chunk),), 1, 0),
        ]
        if path == 1:
            arrivals += [
                ((("own", "x", 0, chunk),), 0, 1),
                ((("own", "y1", 1, 1, chunk),), -1, 1),
                ((("own", "y2", 1, chunk),), 2, 1),
                ((("own", "y1", -1, 1, chunk),), 1, 1),
            ]
        else:
            arrivals += [((("own", "x", row, chunk),), row, 1) for row in (0, -1, 2, 1)]
        for needs, row, other in arrivals:
            event = ("pass", row, other, chunk)
            tasks.append((0, needs, ("core", 1), units, event, 1, ("pass", row, other, chunk)))
    return tasks


def issue_order(tasks):
    users = {}
    for task in tasks:
        for need in task[1]:
            users.setdefault((need, task[0]), []).append(task)

    @functools.lru_cache(None)
    def remaining(task):
        after = [remaining(user) for user in users.get((task[4], task[5]), []) if user[2][0] != "core"]
        return task[3] + 2.0 + max(after, default=0.0)

    step = 0.05
    pending = [[t for t in tasks if t[0] == core] for core in (0, 1)]
    order = ([], [])
    queues = {}
    arrived = {}
    now = 0.0
    while len(arrived) < len(tasks):
        for core in (0, 1):
            ready = [t for t in pending[core] if all(arrived.get((n, core), 1e9) <= now for n in t[1])]
            for task in sorted(ready, key=lambda t: -remaining(t)):
                queue = queues.setdefault((core, task[2]), [])
                if len(queue) < 3:
                    queue.append([task, 1.06 * task[3]])
                    pending[core].remove(task)
                    order[core].append(task)
        for link in {key[1] for key in queues}:
            active = [core for core in (0, 1) if queues.get((core, link))]
            for core in active:
                head = queues[(core, link)][0]
                head[1] -= step / len(active) * (5 if link[0] == "core" else 1)
                if head[1] <= 1e-9:
                    queues[(core, link)].pop(0)
                    arrived[(head[0][4], head[0][5])] = now + step + HOP
        now += step
    return order


def exchange(share_ref, docs_ref, whole_ref, prev_ref, prev_docs_ref, relay_ref, send_sem, recv_sem, local_sem):
    section = lax.axis_index("section")
    shard = lax.axis_index("ctx")
    shards = lax.axis_size("ctx")
    share_heads = share_ref.shape[1]
    y, x_hi = section // 2, section % 2
    core = shard % 2
    x_lo = shard // (shards // 2)
    inner = shard % (shards // 2)

    def along_x(way):
        flips = x_lo == (1 if way == 1 else 0)
        hi = jnp.where(flips, 1 - x_hi, x_hi)
        return hi, {"section": y * 2 + hi, "ctx": (1 - x_lo) * (shards // 2) + inner}

    x_side = {way: along_x(way) for way in (1, -1)}
    y_side = {way: {"section": ((y + way + 4) % 4) * 2 + x_hi, "ctx": shard} for way in (1, -1)}
    later = {"section": section, "ctx": (shard + 1) % shards}
    earlier = {"section": section, "ctx": (shard + shards - 1) % shards}

    barrier = pltpu.get_barrier_semaphore()
    for device in (x_side[1][1], x_side[-1][1], y_side[1], y_side[-1], later, earlier):
        pl.semaphore_signal(barrier, inc=1, device_id=device, device_id_type=MESH)
    pl.semaphore_wait(barrier, 6)

    tasks = all_tasks()
    event_ids = {}
    for task in tasks:
        event_ids.setdefault(task[4], len(event_ids))
    relay_slots, used = {}, 0
    for stream in ("own", "prev"):
        for chunk, entry in enumerate(CHUNKS[stream]):
            for row in (0,) if entry[3] == 1 else (0, -1, 2, 1):
                relay_slots[(stream, row, chunk)] = used
                used += entry[2]

    def row_section(row, hi):
        return ((y + row + 4) % 4) * 2 + hi

    def held(stream, chunk, at):
        kind, head, heads = CHUNKS[stream][chunk][:3]
        ref = whole_ref if stream == "own" else prev_ref
        return ref.at[kind, pl.ds(at * share_heads + head, heads)]

    def own_or_held(stream, chunk, row, hi):
        kind, head, heads = CHUNKS[stream][chunk][:3]
        if row == 0 and hi is x_hi and stream == "own":
            return share_ref.at[kind, pl.ds(head, heads)]
        return held(stream, chunk, row_section(row, hi))

    def relay(stream, row, chunk):
        return relay_ref.at[pl.ds(relay_slots[(stream, row, chunk)], CHUNKS[stream][chunk][2])]

    def ends(what):
        kind = what[0]
        if kind == "ysend":
            _, stream, block, chunk, way = what
            hi = x_hi if block == 0 else 1 - x_hi
            return own_or_held(stream, chunk, 0, hi), held(stream, chunk, row_section(0, hi)), y_side[way]
        if kind == "yfwd":
            _, stream, block, chunk, way = what
            at = row_section(-way, x_hi if block == 0 else 1 - x_hi)
            return held(stream, chunk, at), held(stream, chunk, at), y_side[way]
        if kind == "xsend":
            _, stream, row, chunk, way = what
            return own_or_held(stream, chunk, row, x_hi), relay(stream, row, chunk), x_side[way][1]
        if kind == "xfwd":
            _, stream, row, chunk, way = what
            return relay(stream, row, chunk), held(stream, chunk, row_section(row, x_side[-way][0])), x_side[way][1]
        if kind == "shift":
            part, head, heads = PREV[what[2]][:3]
            return share_ref.at[part, pl.ds(head, heads)], held("prev", what[2], section), later
        _, row, other, chunk = what
        part, head, heads = OWN[chunk][:3]
        at = row_section(row, x_hi if other == 0 else 1 - x_hi)
        target = prev_ref.at[part, pl.ds(at * share_heads + head, heads)]
        return own_or_held("own", chunk, row, x_hi if other == 0 else 1 - x_hi), target, later

    def copy_of(task, number):
        source, target, device = ends(task[6])
        return pltpu.make_async_remote_copy(
            src_ref=source,
            dst_ref=target,
            send_sem=send_sem.at[number],
            recv_sem=recv_sem.at[event_ids[task[4]]],
            device_id=device,
            device_id_type=MESH,
        )

    docs_copy = pltpu.make_async_remote_copy(
        src_ref=docs_ref,
        dst_ref=prev_docs_ref,
        send_sem=local_sem.at[1],
        recv_sem=local_sem.at[2],
        device_id=later,
        device_id_type=MESH,
    )
    docs_copy.start()
    for kind in (0, 1):
        pltpu.make_async_copy(
            share_ref.at[kind], whole_ref.at[kind, pl.ds(section * share_heads, share_heads)], local_sem.at[3 + kind]
        ).start()

    units = {task[4]: task[3] for task in tasks}

    def wait_event(event):
        place = relay_ref.at[pl.ds(0, units[event])]
        pltpu.make_async_copy(place, place, recv_sem.at[event_ids[event]]).wait()

    def run(own_core, order):
        waited = set()
        sent = []
        for number, task in enumerate(order):
            for need in task[1]:
                if need not in waited:
                    waited.add(need)
                    wait_event(need)
            copy = copy_of(task, number)
            copy.start()
            sent.append(copy)
        for task in tasks:
            if task[5] == own_core and task[4] not in waited:
                waited.add(task[4])
                wait_event(task[4])
        for copy in sent:
            copy.wait_send()

    orders = issue_order(tasks)
    for number in (0, 1):
        pl.when(core == number)(functools.partial(run, number, orders[number]))
    docs_copy.wait()
    for kind in (0, 1):
        pltpu.make_async_copy(
            share_ref.at[kind], whole_ref.at[kind, pl.ds(section * share_heads, share_heads)], local_sem.at[3 + kind]
        ).wait()


def gather_cache(share, documents, sections):
    _, heads, rows, dim = share.shape
    tasks = all_tasks()
    relay_units = sum(e[2] * (1 if e[3] == 1 else 4) for e in OWN + PREV)
    sends = max(sum(t[0] == core for t in tasks) for core in (0, 1))
    events = len({t[4] for t in tasks})
    cache = jax.ShapeDtypeStruct((2, heads * sections, rows, dim), share.dtype)
    docs = documents.reshape(-1, 128)
    vmem = pl.BlockSpec(memory_space=pltpu.VMEM)
    hbm = pl.BlockSpec(memory_space=pl.ANY)
    return pl.pallas_call(
        exchange,
        out_shape=(cache, cache, jax.ShapeDtypeStruct(docs.shape, docs.dtype)),
        in_specs=[vmem, vmem],
        out_specs=(hbm, hbm, vmem),
        scratch_shapes=[
            pltpu.VMEM((relay_units, rows, dim), share.dtype),
            pltpu.SemaphoreType.DMA((sends,)),
            pltpu.SemaphoreType.DMA((events,)),
            pltpu.SemaphoreType.DMA((5,)),
        ],
        compiler_params=pltpu.CompilerParams(collective_id=0, has_side_effects=True),
        name="exchange",
    )(share, docs)


def attention(rows, heads, q_ref, cos_ref, sin_ref, ko_ref, kp_ref, vo_ref, vp_ref, qd_ref, kd_ref, o_ref, qf, of, bias):
    window = rows + 128
    blocks = rows // 128
    dim = q_ref.shape[-1]

    @pl.when(pl.program_id(0) == 0)
    def _():
        for block in range(blocks):
            queries = pl.ds(block * 128, 128)
            keys = pl.ds(block * 128, window)
            at_query = lax.broadcasted_iota(jnp.int32, (128, window), 0) + rows
            at_key = lax.broadcasted_iota(jnp.int32, (128, window), 1)
            allowed = jnp.logical_and(kd_ref[:, keys] == qd_ref[queries, :], at_key <= at_query)
            bias[block] = jnp.where(allowed, 0.0, -1e30)

    qf[...] = q_ref[0].astype(jnp.float32)
    factor = dim ** (-0.5) * 1.4426950408889634
    for head in range(heads):
        values = qf[:, head, :]
        turned = values * cos_ref[...] + pltpu.roll(values, dim // 2, 1) * sin_ref[...]
        rotated = turned.astype(jnp.bfloat16)
        for block in range(blocks):
            first = block * 128
            last = first + 128
            query = rotated[first:last]
            contract = (((1,), (1,)), ((), ()))
            scores = jnp.concatenate(
                [
                    lax.dot_general(query, kp_ref[0, head, first:rows], contract, preferred_element_type=jnp.float32),
                    lax.dot_general(query, ko_ref[0, head, 0:last], contract, preferred_element_type=jnp.float32),
                ],
                axis=1,
            )
            scores = scores * factor + bias[block]
            largest = jnp.max(scores, axis=1, keepdims=True)
            weights = jnp.exp2(scores - largest)
            total = jnp.sum(weights, axis=1, keepdims=True)
            probs = weights.astype(jnp.bfloat16)
            mixed = jnp.dot(probs[:, : rows - first], vp_ref[0, head, first:rows], preferred_element_type=jnp.float32)
            mixed += jnp.dot(probs[:, rows - first :], vo_ref[0, head, 0:last], preferred_element_type=jnp.float32)
            of[first:last, head, :] = mixed / total
    o_ref[0] = of[...].astype(jnp.bfloat16)


def attend(queries, whole, prev, cosine, sine, documents, key_docs):
    _, rows, head_count, dim = queries.shape
    group = 8
    window = rows + 128
    q_spec = pl.BlockSpec((1, rows, group, dim), lambda g: (0, 0, g, 0))
    table = pl.BlockSpec((rows, dim), lambda g: (0, 0))
    keys = pl.BlockSpec((1, group, rows, dim), lambda g: (0, g, 0, 0))
    values = pl.BlockSpec((1, group, rows, dim), lambda g: (1, g, 0, 0))
    return pl.pallas_call(
        functools.partial(attention, rows, group),
        grid=(head_count // group,),
        out_shape=jax.ShapeDtypeStruct(queries.shape, queries.dtype),
        in_specs=[
            q_spec,
            table,
            table,
            keys,
            keys,
            values,
            values,
            pl.BlockSpec((rows, 1), lambda g: (0, 0)),
            pl.BlockSpec((1, 2 * rows), lambda g: (0, 0)),
        ],
        out_specs=q_spec,
        scratch_shapes=[
            pltpu.VMEM((rows, group, dim), jnp.float32),
            pltpu.VMEM((rows, group, dim), jnp.float32),
            pltpu.VMEM((rows // 128, 128, window), jnp.float32),
        ],
        name="attend",
    )(queries, cosine, sine, whole, prev, whole, prev, documents[:, None], key_docs[None, :])


def tables(positions, dim):
    half_dim = dim // 2
    exponent = jnp.arange(half_dim, dtype=jnp.float32) * (2.0 / dim)
    inverse = jnp.power(jnp.float32(10000.0), -exponent)
    angles = positions.astype(jnp.float32)[:, None] * inverse[None, :]
    cosine = jnp.cos(angles)
    sine = jnp.sin(angles)
    return jnp.concatenate([cosine, cosine], axis=1), jnp.concatenate([-sine, sine], axis=1)


def body(queries, keys_values, positions, documents):
    dim = queries.shape[-1]
    sections = lax.axis_size("section")
    cosine, sine = tables(positions, dim)
    by_head = jnp.transpose(keys_values, (1, 2, 0, 3))
    keys = by_head[0].astype(jnp.float32)
    swapped = jnp.concatenate([keys[..., dim // 2 :], keys[..., : dim // 2]], axis=-1)
    share = jnp.stack([(keys * cosine + swapped * sine).astype(jnp.bfloat16), by_head[1]], axis=0)
    whole, prev, prev_docs = gather_cache(share, documents, sections)
    at_start = lax.axis_index("ctx") == 0
    key_docs = jnp.concatenate([jnp.where(at_start, -1, prev_docs.reshape(-1)), documents], axis=0)
    return attend(queries, whole, prev, cosine, sine, documents, key_docs)


def solution(mesh):
    placed = (P("section", "ctx", None, None), P("ctx", None, "section", None), P("ctx"), P("ctx"))
    return jax.shard_map(
        body, mesh=mesh, in_specs=placed, out_specs=P("section", "ctx", None, None), check_vma=False
    )
```

time: 345 us -> 145 us (0.42)
  waiting for transfers between devices: 184 us -> 0 us
  Pallas kernels: 0 us -> 136 us
  matrix products: 48.2 us -> 0 us
  local copies, waits for them, and re-layouts: 47.3 us -> 3.91 us
  other arithmetic: 46 us -> 3.81 us
  between operations: 13.5 us -> 0.07 us
  starting transfers between devices: 5.48 us -> 0 us
    pallas_call x0 -> x2, Pallas kernels: none -> 136 us  [the longest x1 93.1 us: gather_cache(): pl.pallas_call(exchange, out_shape=(cache, cache, jax.ShapeDtypeStruct(do...]
    all_gather x1 -> x0, waiting for transfers between devices: 109 us -> none  [body(): whole = lax.all_gather(share, 'section', axis=2, tiled=True)]
    ppermute x2 -> x0, waiting for transfers between devices: 74.6 us -> none  [shifted(): return lax.ppermute(block, axis, route)]
    dot_general x10 -> x0, matrix products: 48.2 us -> none  [the longest x5 33 us: one_group(): jnp.einsum('hqk,khd->qhd', probs, value_part, preferred_element_type=jnp....]
    sub x5 -> x0, other arithmetic: 32.5 us -> none  [one_group(): weights = jnp.exp(scores - largest)]
    slice x2 -> x0, local copies, waits for them, and re-layouts: 14.4 us -> none  [the longest x1 11.1 us: attend(): piece[:, 0]]
    another operation x3 -> x0, local copies, waits for them, and re-layouts: 12.5 us -> none  [the longest x1 10.6 us: split_heads(): return jnp.moveaxis(values.reshape(length, groups, factor, head_dim), 1, 0)]
    unnamed x9 -> x7, local copies, waits for them, and re-layouts: 9.43 us -> 1.51 us
  transfers between devices with their start and end apart: 3 -> 0, of which waited for: 2 -> 0; matrix products, arithmetic and copies ran while one was open for 3% -> 0% of each run, Pallas kernels for 0% -> 0%
where the time goes in v1:
time: 145 us; the launch traced here: 144 us
  Pallas kernels  136 us (94%)
  local copies, waits for them, and re-layouts  3.91 us (3%)
  other arithmetic  3.81 us (3%)
    pallas_call x1, Pallas kernels, gather_cache(): pl.pallas_call(exchange, out_shape=(cache, cache, jax.ShapeDtypeStruct(do...  93.1 us
    pallas_call x1, Pallas kernels, attend(): pl.pallas_call(functools.partial(attention, rows, group), grid=(head_coun...  42.8 us

profile of v1, /device:TPU:2, one launch (start us, length us, event | category | flops | bytes accessed | tf_op | source)
XLA Modules:
  0.0 143.8 jit_solution(3352478210408878)
XLA Ops:
  0.0 0.7 convert_element_type.16
  0.7 1.5 %broadcast_in_dim.17.qd_ref = s32[384,1]{1,0:T(8,128)} reshape(s32[384]{0:T(512)} %param.7) | data formatting | bytes 3072 | tf_op jit(solution)/shard_map/broadcast_in_dim | solution.py:358
  2.2 0.8 fusion.2
  3.0 0.0 copy-start.2
  3.0 0.2 pad_maximum_fusion.1
  3.1 0.0 copy-start
  3.1 0.0 copy-start.1
  3.2 1.5 %copy.9 = bf16[384,2,5,128]{3,0,2,1:T(8,128)(2,1)S(1)} copy(bf16[384,2,5,128]{3,1,2,0:T(2,128)(2,1)} %param.5) | data formatting | bytes 1966080 | tf_op args[1]
  4.7 0.1 convert_bitcast_fusion
  4.8 0.3 slice_bitcast_fusion.1
  5.1 0.4 fusion.1
  5.5 1.0 pad_maximum_fusion.share_ref
  6.5 93.1 %exchange.1 = (bf16[2,40,384,128]{3,2,1,0:T(8,128)(2,1)}, bf16[2,40,384,128]{3,2,1,0:T(8,128)(2,1)}, s32[3,128]{1,0:T(4,128)}) custom-call(bf16[2,5,384,128]{3,2,1,0:T(8,128)(2,1)} %pad_maximum_fusion.share_ref, s32[3,128]{1,0:T(4,128)} %bitcast.14), custom_call_target="tpu_custom_call" | custom-call | tf_op jit(solution)/shard_map/exchange/pallas_call | solution.py:268
  99.7 0.6 select_bitcast_fusion
  100.3 0.0 copy-done.2
  100.3 0.6 broadcast_in_dim.16.kd_ref
  100.9 0.0 copy-done
  100.9 0.0 copy-done.1
  100.9 42.8 %attend.1 = bf16[1,384,40,128]{3,2,1,0:T(8,128)(2,1)} custom-call(bf16[1,384,40,128]{3,2,1,0:T(8,128)(2,1)} %q_ref.1, f32[384,128]{1,0:T(8,128)} %copy-done, f32[384,128]{1,0:T(8,128)} %copy-done.1, bf16[2,40,384,128]{3,2,1,0:T(8,128)(2,1)} %get-tuple-element.8.ko_ref.vo_ref, bf16[2,40,384,128]{3,2,1,0:T(8,128)(2,1)} %get-tuple-element.9.kp_ref.vp_ref, ...), custom_call_target="tpu_custom_call" | custom-call | tf_op jit(solution)/shard_map/attend/pallas_call | solution.py:336
  (2 shorter events, 0.0 us)
Async XLA Ops:
  3.0 97.4 %copy-start.2 = (s32[384]{0:T(512)S(1)}, s32[384]{0:T(512)}, u32[]{:S(2)}) copy-start(s32[384]{0:T(512)} %param.7) | copy-start | bytes 4612
  3.1 97.8 %copy-start = (f32[384,128]{1,0:T(8,128)}, f32[384,128]{1,0:T(8,128)S(1)}, u32[]{:S(2)}) copy-start(f32[384,128]{1,0:T(8,128)S(1)} %get-tuple-element.18.cos_ref) | copy-start | bytes 589828
  3.1 97.8 %copy-start.1 = (f32[384,128]{1,0:T(8,128)}, f32[384,128]{1,0:T(8,128)S(1)}, u32[]{:S(2)}) copy-start(f32[384,128]{1,0:T(8,128)S(1)} %get-tuple-element.19.sin_ref) | copy-start | bytes 589828
